TPU v7x, 32 devices: a whole 2x2x4 slice. The times are simulated.
32 devices in a mesh: tile: 8 (over z, x), ka: 4 (over y, core).
Axes of the slice: x: 2, y: 2, z: 4, core: 2. Of those that a mesh axis runs over, the one named last changes fastest.
Arguments:
- amplitudes: bfloat16 [128, 32, 512], P(('tile', 'ka')), may hold values from -6 to 6
- integrals: bfloat16 [64, 512, 4096], P('tile', None, 'ka'), may hold values from -0.046875 to 0.046875
- slot_block: int32 [64], replicated, may hold values from 0 to 32, as said below
- rest: bfloat16 [128, 4096], P('tile', 'ka'), may hold values from -12 to 12
- occ_energy: float32 [128], P('tile'), may hold values from -2 to -0.5
- vir_energy: float32 [4096], P('ka'), may hold values from 0.5 to 3
Outputs:
- new_amp: bfloat16 [128, 4096], P('tile', 'ka')
Inputs may be any that keep to these rules, and one draw needn't show every extreme that they name: `slot_block`: each of the 32 blocks is stored in exactly one slot; the value 32 marks an empty slot. Slots s*8 to s*8 + 7 belong to owner s along tile; an owner holds 0 to 8 blocks, and some owner holds exactly 8.
All inputs are finite; a program needn't handle non-finite values.
Results may differ from a plain program's by a relative error of at most 0.001.
Values may be sent and summed in bfloat16 or wider, within the bound.
A program may use at most 128 MiB of HBM per device.

v0:
```python
import jax
import jax.numpy as jnp
from jax import lax
from jax.sharding import PartitionSpec as P


def per_device(amplitudes, integrals, slot_block, rest, occ_energy, vir_energy):
    capacity = integrals.shape[0]
    block_width = integrals.shape[1]
    tile_count = slot_block.shape[0] // capacity
    nblocks = amplitudes.shape[1]
    picker = (slot_block[:, None] == jnp.arange(nblocks, dtype=jnp.int32)[None, :]).astype(
        jnp.bfloat16
    )
    outgoing = jnp.einsum(
        "sg,rgb->srb", picker, amplitudes, preferred_element_type=jnp.float32
    ).astype(jnp.bfloat16)
    outgoing = outgoing.reshape(tile_count, capacity, amplitudes.shape[0], block_width)
    routed = lax.all_to_all(outgoing, "tile", split_axis=0, concat_axis=0, tiled=True)
    routed = routed[:, None]
    partial_value = jnp.einsum(
        "tksib,sbn->tkin",
        lax.all_gather(routed, "ka", axis=1, tiled=True),
        integrals,
        preferred_element_type=jnp.float32,
    )
    partial_value = partial_value.reshape(-1, partial_value.shape[-1])
    ladder = lax.psum_scatter(partial_value, "tile", scatter_dimension=0, tiled=True)
    denominator = vir_energy[None, :] - occ_energy[:, None]
    return ((rest.astype(jnp.float32) + ladder) / denominator).astype(jnp.bfloat16)


def solution(mesh):
    in_specs = (
        P(("tile", "ka"), None, None),
        P("tile", None, "ka"),
        P(),
        P("tile", "ka"),
        P("tile"),
        P("ka"),
    )
    out_specs = P("tile", "ka")
    return jax.shard_map(
        per_device, mesh=mesh, in_specs=in_specs, out_specs=out_specs, check_vma=False
    )
```

profile of v0, /device:TPU:0, one launch (start us, length us, event | category | flops | bytes accessed | tf_op | source)
XLA Modules:
  0.0 120.0 jit_solution(10600925300919967446)
XLA Ops:
  6.5 0.0 copy-start
  6.5 0.0 copy-start.2
  6.5 0.0 copy-start.3
  6.5 0.0 copy-start.1
  6.5 0.0 all-gather.3.cloned.1.call-start
  6.6 0.9 copy-done
  7.4 0.9 fusion.5
  8.4 16.1 %all_to_all.5 = bf16[8,8,4,512]{3,1,2,0:T(8,128)(2,1)} all-to-all(bf16[8,8,4,512]{3,1,2,0:T(8,128)(2,1)S(1)} %copy.7), channel_id=1, replica_groups=mesh['tile'=8,'ka'=4] {'tile'}, dimensions={0} | all-to-all | bytes 524288 | tf_op jit(solution)/shard_map/all_to_all | solution.py:19
  24.5 0.0 all-gather.3.cloned.1.call-update
  24.5 0.0 reduce-scatter.2.cloned.1.call-start
  24.6 15.8 %all-gather.3.cloned.1.call-done = bf16[8,32,4,512]{3,1,2,0:T(8,128)(2,1)} async-done(((bf16[8,8,4,512]{3,1,2,0:T(8,128)(2,1)}), bf16[8,32,4,512]{3,1,2,0:T(8,128)(2,1)}) %all-gather.3.cloned.1.call-update) | async-done | bytes 1048592 | tf_op jit(solution)/shard_map/all_gather | solution.py:23
  40.4 7.4 %fusion.2 = f32[8,4,4,1024]{3,2,1,0:T(4,128)S(1)} fusion(bf16[8,512,1024]{2,1,0:T(8,128)(2,1)} %param.7, bf16[8,4,8,4,512]{4,2,1,3,0:T(8,128)(2,1)} %bitcast.16), kind=kOutput, calls=%fused_computation.2 | convolution fusion | flops 1073741824 | bytes 9961472 | tf_op jit(solution)/shard_map/tksib,sbn->tkin/dot_general | solution.py:21
  47.9 1.0 reshape.10
  48.8 0.0 reduce-scatter.2.cloned.1.call-update
  48.9 62.8 %reduce-scatter.2.cloned.1.call-done = f32[16,1024]{1,0:T(8,128)} async-done(((f32[128,1024]{1,0:T(8,128)}), f32[16,1024]{1,0:T(8,128)}) %reduce-scatter.2.cloned.1.call-update) | async-done | bytes 65552 | tf_op jit(solution)/shard_map/reduce_scatter | solution.py:28
  111.6 0.0 copy-done.2
  111.6 0.0 copy-done.3
  111.6 0.0 copy-done.1
  111.6 1.5 %divide_convert_fusion = bf16[16,1024]{1,0:T(8,128)(2,1)} fusion(f32[16,1024]{1,0:T(8,128)} %reduce-scatter.2.cloned.1.call-done, bf16[16,1024]{1,0:T(8,128)(2,1)S(1)} %copy-done.1, f32[16]{0:T(128)S(1)} %copy-done.3, f32[1024]{0:T(1024)S(1)} %copy-done.2), kind=kLoop, calls=%fused_computation.6 | loop fusion | flops 81920 | bytes 135232 | tf_op jit(solution)/shard_map/convert_element_type | solution.py:30
  (1 shorter events, 0.0 us)
Async XLA Ops:
  6.5 0.9 copy-start
  6.5 105.1 %copy-start.2 = (f32[1024]{0:T(1024)S(1)}, f32[1024]{0:T(1024)}, u32[]{:S(2)}) copy-start(f32[1024]{0:T(1024)} %param.11) | copy-start | bytes 12292
  6.5 105.1 %copy-start.3 = (f32[16]{0:T(128)S(1)}, f32[16]{0:T(128)}, u32[]{:S(2)}) copy-start(f32[16]{0:T(128)} %param.10) | copy-start | bytes 196
  6.5 105.1 %copy-start.1 = (bf16[16,1024]{1,0:T(8,128)(2,1)S(1)}, bf16[16,1024]{1,0:T(8,128)(2,1)}, u32[]{:S(2)}) copy-start(bf16[16,1024]{1,0:T(8,128)(2,1)} %param.9) | copy-start | bytes 98308
  6.5 33.9 %all-gather.3.cloned.1.call-start = ((), (), s32[]{:S(2)}) async-start(), calls=%async_computation.3 | async-start | bytes 1310720 | tf_op jit(solution)/shard_map/all_gather | solution.py:23
  24.5 87.1 %reduce-scatter.2.cloned.1.call-start = ((), (), s32[]{:S(2)}) async-start(), calls=%async_computation.2 | async-start | bytes 589824 | tf_op jit(solution)/shard_map/reduce_scatter | solution.py:28
Sparse Core Ops, SparseCore 0:
  24.6 15.7 all-gather.2
  49.0 62.6 reduce-scatter.1
where the time goes:
time: 120 us
  waiting for transfers between devices  78.6 us (65%)
  blocking collectives  16.1 us (13%)
  between operations  13.4 us (11%)
  matrix products  8.37 us (7%)
  local copies, waits for them, and re-layouts  1.86 us (2%)
  other arithmetic  1.54 us (1%)
    reduce_scatter x1, waiting for transfers between devices, per_device(): lax.psum_scatter(partial_value, 'tile', scatter_dimension=0, tiled=True)  62.8 us
    all_to_all x1, blocking collectives, per_device(): lax.all_to_all(outgoing, 'tile', split_axis=0, concat_axis=0, tiled=True)  16.1 us
    all_gather x1, waiting for transfers between devices, per_device(): lax.all_gather(routed, 'ka', axis=1, tiled=True)  15.8 us
    dot_general x1, matrix products, per_device(): jnp.einsum('tksib,sbn->tkin', lax.all_gather(routed, 'ka', axis=1, tiled=...  7.44 us
  transfers between devices with their start and end apart: 2, of which 2 were waited for; matrix products, arithmetic and copies ran while one was open for 0% of the time, Pallas kernels for 0%

commit v1 on v0

--- a/solution.py
+++ b/solution.py
@@ -18,11 +18,49 @@
     outgoing = outgoing.reshape(tile_count, capacity, amplitudes.shape[0], block_width)
     routed = lax.all_to_all(outgoing, "tile", split_axis=0, concat_axis=0, tiled=True)
     routed = routed[:, None]
-    partial_value = jnp.einsum(
-        "tksib,sbn->tkin",
-        lax.all_gather(routed, "ka", axis=1, tiled=True),
-        integrals,
-        preferred_element_type=jnp.float32,
+
+    def find_the_joints(arr, dim_at, original, out_dim):
+        bus_axis = "ka"
+        after, x_next, y_new = (
+            lax.axis_size(bus_axis),
+            lax.axis_index(bus_axis),
+            arr.shape[dim_at],
+        )
+        crops = [(dd, (dd + 1) % after) for dd in range(after)]
+        tray = [(tick, k0) for k0, tick in crops]
+        e_now, known = (lax.ppermute(arr, bus_axis, crops), lax.ppermute(arr, bus_axis, tray))
+        kept_arr = original(arr, x_next * y_new)
+        v_now = kept_arr.shape[out_dim]
+        aux = jnp.zeros(
+            (*kept_arr.shape[:out_dim], after * v_now, *kept_arr.shape[out_dim + 1 :]),
+            kept_arr.dtype,
+        )
+
+        def serve_the_chains(aux, kept_arr, answer):
+            w_next = lax.dynamic_update_slice_in_dim(aux, kept_arr, answer * v_now, axis=out_dim)
+            return w_next
+
+        aux = serve_the_chains(aux, kept_arr, x_next)
+        for i0 in [*range(1, after // 2 + 1)]:
+            tmp, reached = ((x_next - i0) % after, (x_next + i0) % after)
+            work_now = (e_now, known)
+            if i0 < after // 2:
+                e_now, known = (
+                    lax.ppermute(e_now, bus_axis, crops),
+                    lax.ppermute(known, bus_axis, tray),
+                )
+            aux = serve_the_chains(aux, original(work_now[0], tmp * y_new), tmp)
+            if 2 * i0 < after:
+                aux = serve_the_chains(aux, original(work_now[1], reached * y_new), reached)
+        return aux
+
+    partial_value = find_the_joints(
+        routed,
+        1,
+        lambda own_block, offset: jnp.einsum(
+            "tksib,sbn->tkin", own_block, integrals, preferred_element_type=jnp.float32
+        ),
+        1,
     )
     partial_value = partial_value.reshape(-1, partial_value.shape[-1])
     ladder = lax.psum_scatter(partial_value, "tile", scatter_dimension=0, tiled=True)

time: 120 us -> 114 us (0.950)
  blocking collectives: 16.1 us -> 0 us
  starting transfers between devices: 0.08 us -> 7.88 us
  matrix products: 8.37 us -> 10.6 us
  waiting for transfers between devices: 78.6 us -> 77 us
  local copies, waits for them, and re-layouts: 1.86 us -> 3.3 us
    all_to_all x1 -> x0, blocking collectives: 16.1 us -> none  [per_device(): lax.all_to_all(outgoing, 'tile', split_axis=0, concat_axis=0, tiled=True)]
    all_gather x1 -> x0, waiting for transfers between devices: 15.8 us -> none  [per_device(): lax.all_gather(routed, 'ka', axis=1, tiled=True)]
    all_to_all x0 -> x1, waiting for transfers between devices: none -> 8.82 us  [per_device(): lax.all_to_all(outgoing, 'tile', split_axis=0, concat_axis=0, tiled=True)]
    all_to_all x0 -> x1, starting transfers between devices: none -> 7.28 us  [per_device(): lax.all_to_all(outgoing, 'tile', split_axis=0, concat_axis=0, tiled=True)]
    ppermute x0 -> x3, waiting for transfers between devices: none -> 6.78 us  [the longest x1 4.02 us: find_the_joints(): lax.ppermute(e_now, bus_axis, crops)]
    dot_general x1 -> x4, matrix products: 7.44 us -> 9.69 us  [per_device(): jnp.einsum('tksib,sbn->tkin', own_block, integrals, preferred_element_typ...]
    reduce_scatter x1, waiting for transfers between devices: 62.8 us -> 61.4 us  [per_device(): lax.psum_scatter(partial_value, 'tile', scatter_dimension=0, tiled=True)]
  transfers between devices with their start and end apart: 2 -> 5, of which waited for: 2 -> 4; matrix products, arithmetic and copies ran while one was open for 0% -> 8% of each run, Pallas kernels for 0% -> 0%
where the time goes in v1:
time: 114 us
  waiting for transfers between devices  77 us (68%)
  between operations  13.6 us (12%)
  matrix products  10.6 us (9%)
  starting transfers between devices  7.88 us (7%)
  local copies, waits for them, and re-layouts  3.3 us (3%)
  other arithmetic  1.54 us (1%)
    reduce_scatter x1, waiting for transfers between devices, per_device(): lax.psum_scatter(partial_value, 'tile', scatter_dimension=0, tiled=True)  61.4 us
    dot_general x4, matrix products, per_device(): jnp.einsum('tksib,sbn->tkin', own_block, integrals, preferred_element_typ...  9.69 us
    all_to_all x1, waiting for transfers between devices, per_device(): lax.all_to_all(outgoing, 'tile', split_axis=0, concat_axis=0, tiled=True)  8.82 us
    all_to_all x1, starting transfers between devices, per_device(): lax.all_to_all(outgoing, 'tile', split_axis=0, concat_axis=0, tiled=True)  7.28 us
    ppermute x1, waiting for transfers between devices, find_the_joints(): lax.ppermute(e_now, bus_axis, crops)  4.02 us
    ppermute x1, waiting for transfers between devices, find_the_joints(): lax.ppermute(arr, bus_axis, crops)  2.75 us
  transfers between devices with their start and end apart: 5, of which 4 were waited for; matrix products, arithmetic and copies ran while one was open for 8% of the time, Pallas kernels for 0%

profile of v1, /device:TPU:0, one launch (start us, length us, event | category | flops | bytes accessed | tf_op | source)
XLA Modules:
  0.0 113.9 jit_solution(8255471606314252368)
XLA Ops:
  6.5 0.9 copy-done
  7.4 0.9 fusion.8
  8.4 0.7 copy.12
  9.1 7.3 %all-to-all-start = ((bf16[8,8,4,512]{3,1,2,0:T(8,128)(2,1)}), bf16[8,8,4,512]{3,1,2,0:T(8,128)(2,1)S(1)}, u32[]{:S(2)}, u32[]{:S(2)}) async-start(bf16[8,8,4,512]{3,1,2,0:T(8,128)(2,1)} %copy.12), calls=%async_computation | async-start | bytes 524288 | tf_op jit(solution)/shard_map/all_to_all | solution.py:19
  16.4 0.0 reduce-scatter.2.cloned.1.call-start
  16.5 8.8 %all-to-all-done = bf16[8,8,4,512]{3,1,2,0:T(8,128)(2,1)S(1)} async-done(((bf16[8,8,4,512]{3,1,2,0:T(8,128)(2,1)}), bf16[8,8,4,512]{3,1,2,0:T(8,128)(2,1)S(1)}, u32[]{:S(2)}, u32[]{:S(2)}) %all-to-all-start) | async-done | bytes 262176 | tf_op jit(solution)/shard_map/all_to_all | solution.py:19
  25.3 0.1 copy.30
  25.5 0.1 collective-permute-start.1
  25.5 0.5 collective-permute-start
  26.0 5.2 %fusion.9 = f32[8,1,4,1024]{3,0,2,1:T(8,128)S(1)} fusion(bf16[8,512,1024]{2,1,0:T(8,128)(2,1)} %param.7, bf16[8,8,4,512]{3,1,2,0:T(8,128)(2,1)S(1)} %all-to-all-done), kind=kOutput, calls=%fused_computation.10 | convolution fusion | flops 268435456 | bytes 8781824 | tf_op jit(solution)/shard_map/tksib,sbn->tkin/dot_general | solution.py:60
  31.2 0.1 broadcast_in_dim.4
  31.3 0.1 copy_dynamic-update-slice_fusion.3
  31.4 2.8 %collective-permute-done = bf16[8,1,8,4,512]{4,0,2,3,1:T(8,128)(2,1)S(1)} collective-permute-done((bf16[8,1,8,4,512]{4,0,2,3,1:T(8,128)(2,1)S(1)}, bf16[8,1,8,4,512]{4,0,2,3,1:T(8,128)(2,1)S(1)}, u32[]{:S(2)}, u32[]{:S(2)}) %collective-permute-start) | collective-permute-done | bytes 262176 | tf_op jit(solution)/shard_map/ppermute | solution.py:31
  34.2 1.5 %fusion.12 = f32[8,1,4,1024]{3,0,2,1:T(8,128)S(1)} fusion(bf16[8,512,1024]{2,1,0:T(8,128)(2,1)S(1)} %copy-done.1, bf16[8,1,8,4,512]{4,0,2,3,1:T(8,128)(2,1)S(1)} %collective-permute-done), kind=kOutput, calls=%fused_computation.11 | convolution fusion | flops 268435456 | bytes 8781824 | tf_op jit(solution)/shard_map/tksib,sbn->tkin/dot_general | solution.py:60
  35.7 1.5 %fusion.15 = f32[8,1,4,1024]{3,0,2,1:T(8,128)S(1)} fusion(bf16[8,512,1024]{2,1,0:T(8,128)(2,1)S(1)} %copy-done.1, bf16[8,1,8,4,512]{4,0,2,3,1:T(8,128)(2,1)S(1)} %collective-permute-done.1), kind=kOutput, calls=%fused_computation.12 | convolution fusion | flops 268435456 | bytes 8781824 | tf_op jit(solution)/shard_map/tksib,sbn->tkin/dot_general | solution.py:60
  37.3 0.1 copy_dynamic-update-slice_fusion.2
  37.4 0.1 copy_dynamic-update-slice_fusion.1
  37.5 4.0 %collective-permute-done.2 = bf16[8,1,8,4,512]{4,0,2,3,1:T(8,128)(2,1)S(1)} collective-permute-done((bf16[8,1,8,4,512]{4,0,2,3,1:T(8,128)(2,1)S(1)}, bf16[8,1,8,4,512]{4,0,2,3,1:T(8,128)(2,1)S(1)}, u32[]{:S(2)}, u32[]{:S(2)}) %collective-permute-start.2) | collective-permute-done | bytes 262176 | tf_op jit(solution)/shard_map/ppermute | solution.py:49
  41.5 1.5 %fusion.18 = f32[8,1,4,1024]{3,0,2,1:T(8,128)S(1)} fusion(bf16[8,512,1024]{2,1,0:T(8,128)(2,1)S(1)} %copy-done.1, bf16[8,1,8,4,512]{4,0,2,3,1:T(8,128)(2,1)S(1)} %collective-permute-done.2), kind=kOutput, calls=%fused_computation.13 | convolution fusion | flops 268435456 | bytes 8781824 | tf_op jit(solution)/shard_map/tksib,sbn->tkin/dot_general | solution.py:60
  43.0 0.1 copy_dynamic-update-slice_fusion
  43.1 1.0 reshape.28
  44.1 0.0 reduce-scatter.2.cloned.1.call-update
  44.1 61.4 %reduce-scatter.2.cloned.1.call-done = f32[16,1024]{1,0:T(8,128)} async-done(((f32[128,1024]{1,0:T(8,128)}), f32[16,1024]{1,0:T(8,128)}) %reduce-scatter.2.cloned.1.call-update) | async-done | bytes 65552 | tf_op jit(solution)/shard_map/reduce_scatter | solution.py:66
  105.5 1.5 %divide_convert_fusion = bf16[16,1024]{1,0:T(8,128)(2,1)} fusion(f32[16,1024]{1,0:T(8,128)} %reduce-scatter.2.cloned.1.call-done, bf16[16,1024]{1,0:T(8,128)(2,1)S(1)} %copy-done.2, f32[16]{0:T(128)S(1)} %copy-done.4, f32[1024]{0:T(1024)S(1)} %copy-done.3), kind=kLoop, calls=%fused_computation.23 | loop fusion | flops 81920 | bytes 135232 | tf_op jit(solution)/shard_map/convert_element_type | solution.py:68
  (11 shorter events, 0.0 us)
Async XLA Ops:
  6.5 0.9 copy-start
  9.1 16.2 %all-to-all-start = ((bf16[8,8,4,512]{3,1,2,0:T(8,128)(2,1)}), bf16[8,8,4,512]{3,1,2,0:T(8,128)(2,1)S(1)}, u32[]{:S(2)}, u32[]{:S(2)}) async-start(bf16[8,8,4,512]{3,1,2,0:T(8,128)(2,1)} %copy.12), calls=%async_computation | async-start | bytes 524288 | tf_op jit(solution)/shard_map/all_to_all | solution.py:19
  16.4 89.1 %reduce-scatter.2.cloned.1.call-start = ((), (), s32[]{:S(2)}) async-start(), calls=%async_computation.2 | async-start | bytes 589824 | tf_op jit(solution)/shard_map/reduce_scatter | solution.py:66
  25.3 8.9 %copy-start.1 = (bf16[8,512,1024]{2,1,0:T(8,128)(2,1)S(1)}, bf16[8,512,1024]{2,1,0:T(8,128)(2,1)}, u32[]{:S(2)}) copy-start(bf16[8,512,1024]{2,1,0:T(8,128)(2,1)} %param.7) | copy-start | bytes 25165828
  25.5 10.2 %collective-permute-start.1 = (bf16[8,1,8,4,512]{4,0,2,3,1:T(8,128)(2,1)S(1)}, bf16[8,1,8,4,512]{4,0,2,3,1:T(8,128)(2,1)S(1)}, u32[]{:S(2)}, u32[]{:S(2)}) collective-permute-start(bf16[8,1,8,4,512]{4,0,2,3,1:T(8,128)(2,1)S(1)} %bitcast.51), channel_id=1, source_target_pairs={{1,0},{2,1},{3,2},{0,3},{5,4},{6,5},{7,6},{4,7},{9,8},{10,9},{11,1... | collective-permute-start | bytes 786440 | tf_op jit(solution)/shard_map/ppermute | solution.py:31
  25.5 8.6 %collective-permute-start = (bf16[8,1,8,4,512]{4,0,2,3,1:T(8,128)(2,1)S(1)}, bf16[8,1,8,4,512]{4,0,2,3,1:T(8,128)(2,1)S(1)}, u32[]{:S(2)}, u32[]{:S(2)}) collective-permute-start(bf16[8,1,8,4,512]{4,0,2,3,1:T(8,128)(2,1)S(1)} %bitcast.52), channel_id=1, source_target_pairs={{0,1},{1,2},{2,3},{3,0},{4,5},{5,6},{6,7},{7,4},{8,9},{9,10},{10,1... | collective-permute-start | bytes 786440 | tf_op jit(solution)/shard_map/ppermute | solution.py:31
  35.7 5.8 %collective-permute-start.2 = (bf16[8,1,8,4,512]{4,0,2,3,1:T(8,128)(2,1)S(1)}, bf16[8,1,8,4,512]{4,0,2,3,1:T(8,128)(2,1)S(1)}, u32[]{:S(2)}, u32[]{:S(2)}) collective-permute-start(bf16[8,1,8,4,512]{4,0,2,3,1:T(8,128)(2,1)S(1)} %collective-permute-done), channel_id=1, source_target_pairs={{0,1},{1,2},{2,3},{3,0},{4,5},{5,6},{6,7},{7,4},{8,9},{9,10},{10,1... | collective-permute-start | bytes 786440 | tf_op jit(solution)/shard_map/ppermute | solution.py:49
  37.2 68.3 %copy-start.2 = (bf16[16,1024]{1,0:T(8,128)(2,1)S(1)}, bf16[16,1024]{1,0:T(8,128)(2,1)}, u32[]{:S(2)}) copy-start(bf16[16,1024]{1,0:T(8,128)(2,1)} %param.9) | copy-start | bytes 98308
  37.2 68.3 %copy-start.3 = (f32[1024]{0:T(1024)S(1)}, f32[1024]{0:T(1024)}, u32[]{:S(2)}) copy-start(f32[1024]{0:T(1024)} %param.11) | copy-start | bytes 12292
  37.2 68.3 %copy-start.4 = (f32[16]{0:T(128)S(1)}, f32[16]{0:T(128)}, u32[]{:S(2)}) copy-start(f32[16]{0:T(128)} %param.10) | copy-start | bytes 196
Sparse Core Ops, SparseCore 0:
  44.2 61.2 reduce-scatter.1
